TPU v7x, 512 devices: a whole 4x8x8 slice. The times are simulated.
512 devices in a mesh: shard: 64 (over x, z, core), tensor: 8 (over y).
Axes of the slice: x: 4, y: 8, z: 8, core: 2. Of those that a mesh axis runs over, the one named last changes fastest.
Arguments:
- grad: float32 [8, 512, 1024], P(None, 'shard', 'tensor'), may hold values from -500 to 500
- momentum: float32 [8, 512, 1024], P(None, 'shard', 'tensor'), may hold values from -6 to 6
- weight: float32 [8, 512, 1024], P(None, 'shard', 'tensor'), may hold values from -0.625 to 0.625
Outputs:
- new_weight: float32 [8, 512, 1024], P(None, 'shard', 'tensor')
- new_momentum: float32 [8, 512, 1024], P(None, 'shard', 'tensor')
- update: float32 [8, 512, 1024], P(None, 'shard', 'tensor')
All inputs are finite; a program needn't handle non-finite values.
Results may differ from a plain program's by a relative error of at most 0.0078.
Values may be sent and summed in bfloat16 or wider, within the bound.
A program may use at most 64 MiB of HBM per device.

v0:
```python
import math
import jax
import jax.numpy as jnp
from jax import lax
from jax.sharding import PartitionSpec as P

ITERS = 3
mu_decay = 0.95
learn_rate = 0.05
weight_decay = 0.1
update_gain = 0.2
first_coef = 3.4445
second_coef = -4.775
third_coef = 2.0315
epsilon = 1e-07


def regroup(values):
    return lax.all_to_all(
        lax.all_to_all(values, "shard", split_axis=3, concat_axis=1, tiled=True),
        "tensor",
        split_axis=0,
        concat_axis=2,
        tiled=True,
    )


def polish(iterate, gram):
    wide = iterate.astype(jnp.float32)
    squared = jnp.einsum("mrs,mst->mrt", gram, gram, precision=lax.Precision.HIGHEST)
    poly = second_coef * gram + third_coef * squared
    mixed = jnp.einsum("mrs,msc->mrc", poly, wide, precision=lax.Precision.HIGHEST)
    fresh = first_coef * wide + mixed
    return fresh.astype(jnp.bfloat16)


def on_device(grad, momentum, weight):
    mats, rows_local, cols_local = grad.shape
    n_shard = lax.axis_size("shard")
    n_tensor = lax.axis_size("tensor")
    new_momentum = mu_decay * momentum + grad
    advance = lax.optimization_barrier((grad + mu_decay * new_momentum).astype(jnp.bfloat16))
    wide = advance.astype(jnp.float32)
    total = lax.psum(jnp.sum(wide * wide, axis=(1, 2)), ("shard", "tensor"))
    frob = jnp.sqrt(total)[:, None, None] + epsilon
    start = (wide / frob).astype(jnp.bfloat16)
    moved = regroup(start.reshape(mats, rows_local, 1, cols_local))
    group, kv_rows, tensor_cols, thin_cols = moved.shape
    gathered = lax.all_gather(moved, "shard", axis=3, tiled=True)
    iterate = gathered.reshape(group, kv_rows, tensor_cols * n_shard * thin_cols)
    for step in range(ITERS):
        gram = jnp.einsum("mrc,msc->mrs", iterate, iterate, preferred_element_type=jnp.float32)
        iterate = polish(iterate, gram)
    spread = iterate.reshape(group, kv_rows, tensor_cols, n_shard, thin_cols)
    result = lax.dynamic_index_in_dim(spread, lax.axis_index("shard"), 3, keepdims=False)
    back = lax.all_to_all(
        lax.all_to_all(result, "shard", split_axis=1, concat_axis=3, tiled=True),
        "tensor",
        split_axis=2,
        concat_axis=0,
        tiled=True,
    )
    ortho = back.reshape(mats, rows_local, cols_local)
    width = cols_local * n_tensor
    update = update_gain * math.sqrt(width) * ortho.astype(jnp.float32)
    new_weight = weight - learn_rate * (update + weight_decay * weight)
    return (new_weight, new_momentum, update)


def solution(mesh):
    in_specs = (P(None, "shard", "tensor"), P(None, "shard", "tensor"), P(None, "shard", "tensor"))
    out_specs = (P(None, "shard", "tensor"), P(None, "shard", "tensor"), P(None, "shard", "tensor"))
    return jax.shard_map(
        on_device, mesh=mesh, in_specs=in_specs, out_specs=out_specs, check_vma=False
    )
```

profile of v0, /device:TPU:6, one launch (start us, length us, event | category | flops | bytes accessed | tf_op | source)
XLA Modules:
  0.0 277.9 jit_solution(15786168088153653814)
XLA Ops:
  7.2 1.4 add_convert_fusion.3
  8.7 103.3 %psum.7 = f32[8]{0:T(128)S(1)} all-reduce(f32[8]{0:T(128)S(1)} %fusion.4), channel_id=1, replica_groups=mesh['shard'=64,'tensor'=8] {'shard','tensor'}, use_global_device_ids=true, to_apply=%region_1.0 | all-reduce | flops 8 | bytes 64 | tf_op jit(solution)/shard_map/psum | solution.py:44
  112.4 17.5 %all_to_all.63 = bf16[8,8,1,128]{1,0,2,3:T(8,128)(2,1)S(1)} all-to-all(bf16[8,8,1,128]{1,0,2,3:T(8,128)(2,1)S(1)} %copy.53), channel_id=1, replica_groups=mesh['shard'=64,'tensor'=8] {'shard'}, dimensions={3} | all-to-all | bytes 32768 | tf_op jit(solution)/shard_map/all_to_all | solution.py:20
  130.3 13.0 %all_to_all.64 = bf16[8,512,1,2]{1,3,2,0:T(2,128)(2,1)S(1)} all-to-all(bf16[8,512,1,2]{1,3,2,0:T(2,128)(2,1)S(1)} %reshape.105), channel_id=1, replica_groups=mesh['shard'=64,'tensor'=8] {'tensor'}, dimensions={0} | all-to-all | bytes 32768 | tf_op jit(solution)/shard_map/all_to_all | solution.py:19
  143.2 0.6 copy.56
  143.9 74.2 %all-gather.3.cloned.1.call-done = bf16[1,512,8,1,128]{1,2,3,0,4:T(8,128)(2,1)} async-done(((bf16[1,512,8,1,2]{1,2,3,0,4:T(8,128)(2,1)}), bf16[1,512,8,1,128]{1,2,3,0,4:T(8,128)(2,1)}) %all-gather.3.cloned.1.call-update) | async-done | bytes 1048592 | tf_op jit(solution)/shard_map/all_gather | solution.py:49
  218.0 1.9 copy.59
  220.0 0.7 convolution_bitcast_fusion
  220.7 1.9 fusion.2
  222.9 0.7 copy.58
  223.7 1.9 add_convert_fusion.2
  225.5 0.7 fusion.7
  226.3 1.9 fusion.1
  228.2 1.9 add_convert_fusion.1
  230.1 0.7 fusion.8
  230.8 1.9 fusion
  232.7 1.9 add_convert_fusion
  234.6 0.5 copy.60
  235.2 0.4 reshape.100
  235.8 19.2 %all_to_all.65 = bf16[1,512,8,2]{2,3,0,1:T(2,128)(2,1)S(1)} all-to-all(bf16[1,512,8,2]{2,3,0,1:T(2,128)(2,1)S(1)} %copy.62), channel_id=1, replica_groups=mesh['shard'=64,'tensor'=8] {'shard'}, dimensions={1} | all-to-all | bytes 32768 | tf_op jit(solution)/shard_map/all_to_all | solution.py:57
  255.1 0.5 copy.69
  255.6 0.4 copy.64
  256.1 14.3 %all_to_all.66 = bf16[1,8,8,128]{3,1,0,2:T(8,128)(2,1)S(1)} all-to-all(bf16[1,8,8,128]{3,1,0,2:T(8,128)(2,1)S(1)} %copy.65), channel_id=1, replica_groups=mesh['shard'=64,'tensor'=8] {'tensor'}, dimensions={2} | all-to-all | bytes 32768 | tf_op jit(solution)/shard_map/all_to_all | solution.py:56
  270.4 0.6 multiply_subtract_fusion
  (16 shorter events, 1.5 us)
Async XLA Ops:
  7.2 210.9 %all-gather.3.cloned.1.call-start = ((), (), s32[]{:S(2)}) async-start(), calls=%async_computation.4 | async-start | bytes 1064960 | tf_op jit(solution)/shard_map/all_gather | solution.py:49
  220.7 1.9 copy-start
  235.6 34.8 %copy-start.1 = (f32[8,8,128]{2,1,0:T(8,128)S(1)}, f32[8,8,128]{2,1,0:T(8,128)}, u32[]{:S(2)}) copy-start(f32[8,8,128]{2,1,0:T(8,128)} %param.5) | copy-start | bytes 98308
Sparse Core Ops, SparseCore 0:
  144.0 74.0 all-gather.2
where the time goes:
time: 278 us
  blocking collectives  167 us (60%)
  waiting for transfers between devices  74.2 us (27%)
  between operations  14.2 us (5%)
  matrix products  13.5 us (5%)
  local copies, waits for them, and re-layouts  6.34 us (2%)
    psum x1, blocking collectives, on_device(): total = lax.psum(jnp.sum(wide * wide, axis=(1, 2)), ('shard', 'tensor'))  103 us
    all_gather x1, waiting for transfers between devices, on_device(): gathered = lax.all_gather(moved, 'shard', axis=3, tiled=True)  74.2 us
    all_to_all x1, blocking collectives, on_device(): lax.all_to_all(result, 'shard', split_axis=1, concat_axis=3, tiled=True)  19.2 us
    all_to_all x1, blocking collectives, regroup(): lax.all_to_all(values, 'shard', split_axis=3, concat_axis=1, tiled=True)  17.5 us
    all_to_all x1, blocking collectives, on_device(): lax.all_to_all(lax.all_to_all(result, 'shard', split_axis=1, concat_axis=...  14.3 us
    all_to_all x1, blocking collectives, regroup(): lax.all_to_all(lax.all_to_all(values, 'shard', split_axis=3, concat_axis=...  13 us
    dot_general x3, matrix products, polish(): jnp.einsum('mrs,mst->mrt', gram, gram, precision=lax.Precision.HIGHEST)  5.7 us
    dot_general x3, matrix products, polish(): jnp.einsum('mrs,msc->mrc', poly, wide, precision=lax.Precision.HIGHEST)  5.58 us
  transfers between devices with their start and end apart: 1, of which 1 were waited for; matrix products, arithmetic and copies ran while one was open for 0% of the time, Pallas kernels for 0%

commit v1 on v0

--- a/solution.py
+++ b/solution.py
@@ -46,7 +46,9 @@
     start = (wide / frob).astype(jnp.bfloat16)
     moved = regroup(start.reshape(mats, rows_local, 1, cols_local))
     group, kv_rows, tensor_cols, thin_cols = moved.shape
-    gathered = lax.all_gather(moved, "shard", axis=3, tiled=True)
+    gathered = jnp.concatenate(
+        lax.all_to_all(jnp.stack([moved] * lax.axis_size("shard")), "shard", 0, 0), axis=3
+    )
     iterate = gathered.reshape(group, kv_rows, tensor_cols * n_shard * thin_cols)
     for step in range(ITERS):
         gram = jnp.einsum("mrc,msc->mrs", iterate, iterate, preferred_element_type=jnp.float32)

time: 278 us -> 222 us (0.80)
  waiting for transfers between devices: 74.2 us -> 26.6 us
  between operations: 14.2 us -> 0.8 us
  starting transfers between devices: 0.04 us -> 6.46 us
  blocking collectives: 167 us -> 163 us
    all_gather x1 -> x0, waiting for transfers between devices: 74.2 us -> none  [on_device(): gathered = lax.all_gather(moved, 'shard', axis=3, tiled=True)]
    all_to_all x0 -> x1, waiting for transfers between devices: none -> 26.6 us  [on_device(): lax.all_to_all(jnp.stack([moved] * lax.axis_size('shard')), 'shard', 0, 0)]
    all_to_all x0 -> x1, starting transfers between devices: none -> 6.46 us  [on_device(): lax.all_to_all(jnp.stack([moved] * lax.axis_size('shard')), 'shard', 0, 0)]
    all_to_all x1, blocking collectives: 14.3 us -> 10.1 us  [on_device(): lax.all_to_all(lax.all_to_all(result, 'shard', split_axis=1, concat_axis=...]
    another operation x0 -> x3, local copies, waits for them, and re-layouts: none -> 3.16 us  [the longest x1 2 us: on_device(): jnp.stack([moved] * lax.axis_size('shard'))]
where the time goes in v1:
time: 222 us
  blocking collectives  163 us (73%)
  waiting for transfers between devices  26.6 us (12%)
  matrix products  14.7 us (7%)
  local copies, waits for them, and re-layouts  7.58 us (3%)
  starting transfers between devices  6.46 us (3%)
  other arithmetic  2.27 us (1%)
    psum x1, blocking collectives, on_device(): total = lax.psum(jnp.sum(wide * wide, axis=(1, 2)), ('shard', 'tensor'))  103 us
    all_to_all x1, waiting for transfers between devices, on_device(): lax.all_to_all(jnp.stack([moved] * lax.axis_size('shard')), 'shard', 0, 0)  26.6 us
    all_to_all x1, blocking collectives, on_device(): lax.all_to_all(result, 'shard', split_axis=1, concat_axis=3, tiled=True)  19.4 us
    all_to_all x1, blocking collectives, regroup(): lax.all_to_all(values, 'shard', split_axis=3, concat_axis=1, tiled=True)  17.5 us
    all_to_all x1, blocking collectives, regroup(): lax.all_to_all(lax.all_to_all(values, 'shard', split_axis=3, concat_axis=...  13 us
    all_to_all x1, blocking collectives, on_device(): lax.all_to_all(lax.all_to_all(result, 'shard', split_axis=1, concat_axis=...  10.1 us
    all_to_all x1, starting transfers between devices, on_device(): lax.all_to_all(jnp.stack([moved] * lax.axis_size('shard')), 'shard', 0, 0)  6.46 us
    dot_general x3, matrix products, polish(): jnp.einsum('mrs,mst->mrt', gram, gram, precision=lax.Precision.HIGHEST)  5.7 us
  transfers between devices with their start and end apart: 1, of which 1 were waited for; matrix products, arithmetic and copies ran while one was open for 0% of the time, Pallas kernels for 0%

profile of v1, /device:TPU:6, one launch (start us, length us, event | category | flops | bytes accessed | tf_op | source)
XLA Modules:
  0.0 221.9 jit_solution(9073263057486580648)
XLA Ops:
  0.6 1.4 add_convert_fusion.3
  2.2 103.3 %psum.7 = f32[8]{0:T(128)S(1)} all-reduce(f32[8]{0:T(128)S(1)} %fusion.5), channel_id=1, replica_groups=mesh['shard'=64,'tensor'=8] {'shard','tensor'}, use_global_device_ids=true, to_apply=%region_1.0 | all-reduce | flops 8 | bytes 64 | tf_op jit(solution)/shard_map/psum | solution.py:44
  105.8 17.5 %all_to_all.65 = bf16[8,8,1,128]{1,0,2,3:T(8,128)(2,1)S(1)} all-to-all(bf16[8,8,1,128]{1,0,2,3:T(8,128)(2,1)S(1)} %copy.37), channel_id=1, replica_groups=mesh['shard'=64,'tensor'=8] {'shard'}, dimensions={3} | all-to-all | bytes 32768 | tf_op jit(solution)/shard_map/all_to_all | solution.py:20
  123.7 13.0 %all_to_all.66 = bf16[8,512,1,2]{1,3,2,0:T(2,128)(2,1)S(1)} all-to-all(bf16[8,512,1,2]{1,3,2,0:T(2,128)(2,1)S(1)} %reshape.107), channel_id=1, replica_groups=mesh['shard'=64,'tensor'=8] {'tensor'}, dimensions={0} | all-to-all | bytes 32768 | tf_op jit(solution)/shard_map/all_to_all | solution.py:19
  136.6 2.0 stack.5
  138.6 6.5 %all-to-all-start.2 = ((bf16[64,1,512,8,2]{2,4,3,1,0:T(2,128)(2,1)}), bf16[64,1,512,8,2]{2,4,3,1,0:T(2,128)(2,1)S(1)}, u32[]{:S(2)}, u32[]{:S(2)}) async-start(bf16[64,1,512,8,2]{2,4,3,1,0:T(2,128)(2,1)} %stack.5), calls=%async_computation.2 | async-start | bytes 2097152 | tf_op jit(solution)/shard_map/all_to_all | solution.py:50
  145.1 26.6 %all-to-all-done.2 = bf16[64,1,512,8,2]{2,4,3,1,0:T(2,128)(2,1)S(1)} async-done(((bf16[64,1,512,8,2]{2,4,3,1,0:T(2,128)(2,1)}), bf16[64,1,512,8,2]{2,4,3,1,0:T(2,128)(2,1)S(1)}, u32[]{:S(2)}, u32[]{:S(2)}) %all-to-all-start.2) | async-done | bytes 1048608 | tf_op jit(solution)/shard_map/all_to_all | solution.py:50
  171.7 0.6 copy.60
  172.3 1.1 copy.41
  173.9 2.0 convolution_bitcast_fusion
  175.8 1.9 fusion.2
  177.7 0.7 copy.42
  178.4 1.9 add_convert_fusion.2
  180.3 0.7 fusion.8
  181.0 1.9 fusion.1
  183.0 1.9 add_convert_fusion.1
  184.8 0.7 fusion.9
  185.6 1.9 fusion
  187.5 1.9 add_convert_fusion
  189.4 0.5 copy.43
  190.6 19.4 %all_to_all.67 = bf16[1,512,8,2]{2,3,0,1:T(2,128)(2,1)S(1)} all-to-all(bf16[1,512,8,2]{2,3,0,1:T(2,128)(2,1)S(1)} %copy.45), channel_id=1, replica_groups=mesh['shard'=64,'tensor'=8] {'shard'}, dimensions={1} | all-to-all | bytes 32768 | tf_op jit(solution)/shard_map/all_to_all | solution.py:59
  210.0 0.5 copy.53
  211.1 10.1 %all_to_all.68 = bf16[1,8,8,128]{3,1,0,2:T(8,128)(2,1)S(1)} all-to-all(bf16[1,8,8,128]{3,1,0,2:T(8,128)(2,1)S(1)} %copy.48), channel_id=1, replica_groups=mesh['shard'=64,'tensor'=8] {'tensor'}, dimensions={2} | all-to-all | bytes 32768 | tf_op jit(solution)/shard_map/all_to_all | solution.py:58
  221.2 0.6 multiply_subtract_fusion
  (14 shorter events, 2.4 us)
Async XLA Ops:
  138.6 33.1 %all-to-all-start.2 = ((bf16[64,1,512,8,2]{2,4,3,1,0:T(2,128)(2,1)}), bf16[64,1,512,8,2]{2,4,3,1,0:T(2,128)(2,1)S(1)}, u32[]{:S(2)}, u32[]{:S(2)}) async-start(bf16[64,1,512,8,2]{2,4,3,1,0:T(2,128)(2,1)} %stack.5), calls=%async_computation.2 | async-start | bytes 2097152 | tf_op jit(solution)/shard_map/all_to_all | solution.py:50
  190.4 30.8 %copy-start = (f32[8,8,128]{2,1,0:T(8,128)S(1)}, f32[8,8,128]{2,1,0:T(8,128)}, u32[]{:S(2)}) copy-start(f32[8,8,128]{2,1,0:T(8,128)} %param.5) | copy-start | bytes 98308
